TPU v7x, 32 devices: a whole 2x2x4 slice. The times are simulated.
32 devices in a mesh: seq: 8 (over z, y), tp: 4 (over x, core).
Axes of the slice: x: 2, y: 2, z: 4, core: 2. Of those that a mesh axis runs over, the one named last changes fastest.
Arguments:
- x_in: bfloat16 [1024, 8192], P('seq', 'tp'), may hold values from -6 to 6
- gate_in: bfloat16 [1024, 8192], P('seq', 'tp'), may hold values from -6 to 6
- conv_weight: float32 [4, 8192], P(None, 'tp'), may hold values from -3 to 3
- conv_bias: float32 [8192], P('tp'), may hold values from -0.5 to 0.5
- x_weight: bfloat16 [8192, 544], P('tp'), may hold values from -0.0625 to 0.0625
- dt_weight: bfloat16 [512, 8192], P(None, 'tp'), may hold values from -0.25 to 0.25
- dt_bias: float32 [8192], P('tp'), may hold values from -5 to -2.5
- decay_rate: float32 [8192, 16], P('tp'), may hold values from 0 to 4
- skip_gain: float32 [8192], P('tp'), may hold values from 0.5 to 1.5
- out_weight: bfloat16 [8192, 4096], P('tp'), may hold values from -0.0625 to 0.0625
- residual_in: bfloat16 [1024, 4096], P(('seq', 'tp')), may hold values from -36 to 36
- norm_gain: float32 [4096], replicated, may hold values from 0.1 to 1.9
- expert_ids: int32 [1024, 2], P(('seq', 'tp')), may hold values from 0 to 7, all different within a row; in each aligned block of 32 rows (0 to 31, 32 to 63, ...) at most 12 rows name the same one
- gate_prob: float32 [1024, 2], P(('seq', 'tp')), may hold values from 0.1 to 1
- up_weight: bfloat16 [4096, 98304], P(None, ('seq', 'tp')), may hold values from -0.09375 to 0.09375
- down_weight: bfloat16 [98304, 4096], P(('seq', 'tp')), may hold values from -0.0546875 to 0.0546875
Outputs:
- mixer_out: bfloat16 [1024, 4096], P(('seq', 'tp'))
- layer_out: bfloat16 [1024, 4096], P(('seq', 'tp'))
Inputs may be any that keep to these rules, and one draw needn't show every extreme that they name: `expert_ids`: each row names two different experts. In each device's aligned block of 32 rows no expert is named by more than 12 rows, a bound that some block reaches.
All inputs are finite; a program needn't handle non-finite values.
Results may differ from a plain program's by a relative error of at most 0.007.
Values may be sent and summed in bfloat16 or wider, within the bound.
A program may use at most 192 MiB of HBM per device.

v0:
```python
import jax
import jax.numpy as jnp
from jax import lax
from jax.sharding import PartitionSpec as P

STATE = 16
DTRANK = 512
EXPERTS = 8


def shifted(value, axis, steps):
    count = lax.axis_size(axis)
    initial, last = (max(0, -steps), min(count, count - steps))
    return lax.ppermute(value, axis, [(source, source + steps) for source in range(initial, last)])


def prefix(part, axis, combine, identity):
    place = lax.axis_index(axis)
    gathered = jax.tree.map(lambda a: lax.all_gather(a, axis), part)
    state = jax.tree.map(lambda a, e: jnp.zeros_like(a) + jnp.asarray(e, a.dtype), part, identity)

    def one(hop, state):
        return combine(
            state, jax.tree.map(lambda a: lax.dynamic_index_in_dim(a, hop, 0, False), gathered)
        )

    return lax.fori_loop(0, place, one, state)


def chain_join(earlier, later):
    return (earlier[0] * later[0], later[0] * earlier[1] + later[1])


def recur_blocks(start_state, step_cols, drive_cols, entry_cols, readout_cols, negative_rate):

    def advance(carried, columns):
        step_row, drive_row, entry_row, readout_row = columns
        carried = (
            jnp.exp(step_row[:, None, :] * negative_rate[None]) * carried
            + entry_row[:, :, None] * drive_row[:, None, :]
        )
        return (carried, jnp.sum(readout_row[:, :, None] * carried, axis=1))

    return lax.scan(advance, start_state, (step_cols, drive_cols, entry_cols, readout_cols))


def by_position(values, blocks, span):
    return values.reshape(blocks, span, values.shape[1]).transpose(1, 0, 2)


def expert_share(arrived_flat, up_weight, down_weight):
    hidden = jax.nn.silu(
        jnp.dot(arrived_flat, up_weight, preferred_element_type=jnp.float32)
    ).astype(jnp.bfloat16)
    return jnp.dot(hidden, down_weight, preferred_element_type=jnp.float32).astype(jnp.bfloat16)


def per_device(
    x_in,
    gate_in,
    conv_weight,
    conv_bias,
    x_weight,
    dt_weight,
    dt_bias,
    decay_rate,
    skip_gain,
    out_weight,
    residual_in,
    norm_gain,
    expert_ids,
    gate_prob,
    up_weight,
    down_weight,
):
    tokens, channels = x_in.shape
    width = out_weight.shape[1]
    reach = conv_weight.shape[0] - 1
    rim_rows = shifted(x_in[tokens - reach :], "seq", 1)
    padded = jnp.concatenate([rim_rows, x_in], axis=0).astype(jnp.float32)
    conv_out = conv_bias[None, :] + sum(
        (
            conv_weight[offset][None, :] * padded[offset : offset + tokens]
            for offset in range(reach + 1)
        )
    )
    inner = jax.nn.silu(conv_out).astype(jnp.bfloat16)
    projected = lax.psum(jnp.dot(inner, x_weight, preferred_element_type=jnp.float32), "tp")
    dt_low = projected[:, :DTRANK].astype(jnp.bfloat16)
    entry_rows = projected[:, DTRANK : DTRANK + STATE]
    readout_rows = projected[:, DTRANK + STATE :]
    step_size = jax.nn.softplus(
        jnp.dot(dt_low, dt_weight, preferred_element_type=jnp.float32) + dt_bias[None, :]
    )
    drive = step_size * inner.astype(jnp.float32)
    negative_rate = -decay_rate.T
    span = 16
    blocks = tokens // span
    step_cols = by_position(step_size, blocks, span)
    drive_cols = by_position(drive, blocks, span)
    entry_cols = by_position(entry_rows, blocks, span)
    readout_cols = by_position(readout_rows, blocks, span)
    zero_blocks = jnp.zeros((blocks, STATE, channels), jnp.float32)
    block_ends, local_out = recur_blocks(
        zero_blocks, step_cols, drive_cols, entry_cols, readout_cols, negative_rate
    )
    block_decay = jnp.exp(negative_rate[None] * jnp.sum(step_cols, axis=0)[:, None, :])
    decay_through, state_through = lax.associative_scan(
        chain_join, (block_decay, block_ends), axis=0
    )
    ones_state = jnp.ones((STATE, channels), jnp.float32)
    zeros_state = jnp.zeros((STATE, channels), jnp.float32)
    entering = prefix(
        (decay_through[-1], state_through[-1]), "seq", chain_join, (ones_state, zeros_state)
    )[1]
    decay_before = jnp.concatenate([ones_state[None], decay_through[:-1]], axis=0)
    state_before = jnp.concatenate([zeros_state[None], state_through[:-1]], axis=0)
    block_starts = decay_before * entering[None] + state_before
    ssm_cols = recur_blocks(
        block_starts, step_cols, drive_cols, entry_cols, readout_cols, negative_rate
    )[1]
    ssm = ssm_cols.transpose(1, 0, 2).reshape(tokens, channels)
    mixed = (
        (ssm + skip_gain[None, :] * inner.astype(jnp.float32))
        * jax.nn.silu(gate_in.astype(jnp.float32))
    ).astype(jnp.bfloat16)
    rows = tokens // lax.axis_size("tp")
    mixer_sum = lax.psum_scatter(
        jnp.dot(mixed, out_weight, preferred_element_type=jnp.float32),
        "tp",
        scatter_dimension=0,
        tiled=True,
    )
    mixer_out = (mixer_sum + residual_in.astype(jnp.float32)).astype(jnp.bfloat16)
    mixer_wide = mixer_out.astype(jnp.float32)
    normed = (
        mixer_wide
        * lax.rsqrt(jnp.mean(mixer_wide * mixer_wide, axis=1, keepdims=True) + 1e-06)
        * norm_gain[None, :]
    ).astype(jnp.bfloat16)
    seq_count = lax.axis_size("seq")
    devices = seq_count * lax.axis_size("tp")
    seq_group = seq_count // EXPERTS
    capacity = 3 * rows // EXPERTS
    chosen = expert_ids.reshape(-1)
    expert_hits = (chosen[:, None] == jnp.arange(EXPERTS, dtype=jnp.int32)[None, :]).astype(
        jnp.int32
    )
    earlier_hits = jnp.cumsum(expert_hits, axis=0) - expert_hits
    slot_index = jnp.sum(earlier_hits * expert_hits, axis=1)
    target = chosen * capacity + slot_index
    placing = (jnp.arange(EXPERTS * capacity, dtype=jnp.int32)[:, None] == target[None, :]).astype(
        jnp.bfloat16
    )
    placing = jnp.sum(placing.reshape(EXPERTS * capacity, rows, 2), axis=2)
    slots_out = (
        jnp.dot(placing, normed, preferred_element_type=jnp.float32)
        .astype(jnp.bfloat16)
        .reshape(EXPERTS, capacity, width)
    )
    along_seq = jnp.repeat(slots_out, seq_group, axis=0)
    arrived_seq = lax.all_to_all(along_seq, "seq", split_axis=0, concat_axis=0, tiled=True)
    arrived_all = lax.all_gather(
        arrived_seq.reshape(1, seq_count * capacity, width), "tp", axis=0, tiled=True
    )
    arrived_flat = arrived_all.reshape(devices * capacity, width)
    summed = lax.psum_scatter(
        expert_share(arrived_flat, up_weight, down_weight).astype(jnp.float32).astype(jnp.bfloat16),
        "tp",
        scatter_dimension=0,
        tiled=True,
    ).astype(jnp.float32)
    home = lax.all_to_all(
        summed.reshape(seq_count, capacity, width).astype(jnp.bfloat16),
        "seq",
        split_axis=0,
        concat_axis=0,
        tiled=True,
    ).astype(jnp.float32)
    expert_out = jnp.sum(home.reshape(EXPERTS, seq_group, capacity, width), axis=1).reshape(
        EXPERTS * capacity, width
    )
    picked = jnp.take(expert_out, target, axis=0).reshape(rows, 2, width)
    layer_out = (mixer_wide + jnp.sum(picked * gate_prob[:, :, None], axis=1)).astype(jnp.bfloat16)
    return (mixer_out, layer_out)


def solution(mesh):
    return jax.shard_map(
        per_device,
        mesh=mesh,
        in_specs=(
            P("seq", "tp"),
            P("seq", "tp"),
            P(None, "tp"),
            P("tp"),
            P("tp", None),
            P(None, "tp"),
            P("tp"),
            P("tp", None),
            P("tp"),
            P("tp", None),
            P(("seq", "tp"), None),
            P(),
            P(("seq", "tp"), None),
            P(("seq", "tp"), None),
            P(None, ("seq", "tp")),
            P(("seq", "tp"), None),
        ),
        out_specs=(P(("seq", "tp"), None), P(("seq", "tp"), None)),
        check_vma=False,
    )
```

profile of v0, /device:TPU:0, one launch (start us, length us, event | category | flops | bytes accessed | tf_op | source)
XLA Modules:
  0.0 464.8 jit_solution(15491746981362353329)
XLA Ops:
  8.1 4.9 %collective-permute-start = (bf16[3,2048]{1,0:T(4,128)(2,1)S(1)}, bf16[3,2048]{1,0:T(4,128)(2,1)S(1)}, u32[]{:S(2)}, u32[]{:S(2)}) collective-permute-start(bf16[3,2048]{1,0:T(4,128)(2,1)S(1)} %slice.130), channel_id=1, source_target_pairs={{0,4},{4,8},{8,12},{12,16},{16,20},{20,24},{24,28},{1,5},{5,9},{9,... | collective-permute-start | bytes 36872 | tf_op jit(solution)/shard_map/ppermute | solution.py:14
  19.5 33.8 %all-reduce.16.cloned.1.call-done = f32[128,544]{0,1:T(8,128)} async-done(((f32[128,544]{0,1:T(8,128)}), f32[128,544]{0,1:T(8,128)}) %all-reduce.16.cloned.1.call-update) | async-done | bytes 278544 | tf_op jit(solution)/shard_map/psum | solution.py:88
  53.3 2.7 convert_multiply_fusion.2
  56.6 2.6 copy_bitcast_fusion
  60.6 22.9 %while.37 = (s32[]{:T(128)}, f32[8,16,2048]{2,1,0:T(8,128)S(1)}, f32[16,8,2048]{2,1,0:T(8,128)}, f32[16,2048]{1,0:T(8,128)S(1)}, f32[16,8,16]{2,1,0:T(8,128)S(1)...) while((s32[]{:T(128)}, f32[8,16,2048]{2,1,0:T(8,128)S(1)}, f32[16,8,2048]{2,1,0:T(8,128)}, ...), condition=%wide.region_3.4_spmd.clone, body=%wide.region_2.3_spmd.clone.sunk | while | flops 1310723 | bytes 2623079 | solution.py:44
  87.4 2.4 pad.48
  94.4 4.2 pad.102
  100.1 2.4 pad.42
  102.6 2.4 pad.43
  123.3 4.2 pad.44
  131.9 20.2 %all-gather.6.cloned.1.call-done = f32[8,16,2048]{2,1,0:T(8,128)} async-done(((f32[1,16,2048]{2,1,0:T(8,128)}), f32[8,16,2048]{2,1,0:T(8,128)}) %all-gather.6.cloned.1.call-update) | async-done | bytes 1048592 | tf_op jit(solution)/shard_map/all_gather | solution.py:19
  152.1 41.6 %all-gather.4.cloned.1.call-done = f32[8,16,2048]{2,1,0:T(8,128)} async-done(((f32[1,16,2048]{2,1,0:T(8,128)}), f32[8,16,2048]{2,1,0:T(8,128)}) %all-gather.4.cloned.1.call-update) | async-done | bytes 1048592 | tf_op jit(solution)/shard_map/all_gather | solution.py:19
  195.3 36.9 %while.36 = (s32[]{:T(128)}, f32[8,16,2048]{2,1,0:T(8,128)S(1)}, f32[16,8,2048]{2,1,0:T(8,128)}, f32[16,8,2048]{2,1,0:T(8,128)}, f32[16,2048]{1,0:T(8,128)S(1)},...) while((s32[]{:T(128)}, f32[8,16,2048]{2,1,0:T(8,128)S(1)}, ...), condition=%wide.region_8.9_spmd, body=%wide.region_6.8_spmd.sunk | while | flops 1556482 | bytes 2821733 | solution.py:44
  235.1 9.5 %fusion.40 = f32[128,4096]{1,0:T(8,128)} fusion(bf16[128,2048]{1,0:T(8,128)(2,1)S(1)} %fusion.4, bf16[2048,4096]{1,0:T(8,128)(2,1)} %param.31), kind=kOutput, calls=%fused_computation.108 | convolution fusion | flops 2147483648 | bytes 19398656 | tf_op jit(solution)/shard_map/dot_general | solution.py:129
  245.6 36.9 %reduce-scatter.3.cloned.1.call-done = f32[32,4096]{1,0:T(8,128)} async-done(((f32[128,4096]{1,0:T(8,128)}), f32[32,4096]{1,0:T(8,128)}) %reduce-scatter.3.cloned.1.call-update) | async-done | bytes 524304 | tf_op jit(solution)/shard_map/reduce_scatter | solution.py:128
  285.0 31.1 %all_to_all.10 = bf16[8,12,4096]{2,1,0:T(8,128)(2,1)S(1)} all-to-all(bf16[8,12,4096]{2,1,0:T(8,128)(2,1)S(1)} %reshape_broadcast_in_dim_reshape.3), channel_id=1, replica_groups=mesh['seq'=8,'tp'=4] {'seq'}, dimensions={0} | all-to-all | bytes 1572864 | tf_op jit(solution)/shard_map/all_to_all | solution.py:162
  317.4 26.5 %all-gather.8.cloned.1.call-done = bf16[4,96,4096]{2,1,0:T(8,128)(2,1)} async-done(((bf16[1,96,4096]{2,1,0:T(8,128)(2,1)}), bf16[4,96,4096]{2,1,0:T(8,128)(2,1)}) %all-gather.8.cloned.1.call-update) | async-done | bytes 3145744 | tf_op jit(solution)/shard_map/all_gather | solution.py:163
  343.9 16.0 %multiply_convert_fusion.5 = bf16[384,3072]{1,0:T(8,128)(2,1)S(1)} fusion(bf16[384,4096]{1,0:T(8,128)(2,1)} %bitcast.97, bf16[4096,3072]{1,0:T(8,128)(2,1)} %param.36), kind=kOutput, calls=%fused_computation.16.clone.clone.1 | convolution fusion | flops 9669574656 | bytes 30670848 | tf_op jit(solution)/shard_map/dot_general | solution.py:53
  360.0 15.9 %convolution_convert_fusion = bf16[384,4096]{1,0:T(8,128)(2,1)} fusion(bf16[3072,4096]{1,0:T(8,128)(2,1)} %param.37, bf16[384,3072]{1,0:T(8,128)(2,1)S(1)} %multiply_convert_fusion.5), kind=kOutput, calls=%fused_computation.15 | convolution fusion | flops 9665249280 | bytes 30670848 | tf_op jit(solution)/shard_map/dot_general | solution.py:55
  375.9 38.1 %reduce-scatter.5.cloned.1.call-done = bf16[96,4096]{1,0:T(8,128)(2,1)} async-done(((bf16[384,4096]{1,0:T(8,128)(2,1)}), bf16[96,4096]{1,0:T(8,128)(2,1)}) %reduce-scatter.5.cloned.1.call-update) | async-done | bytes 786448 | tf_op jit(solution)/shard_map/reduce_scatter | solution.py:167
  416.2 5.5 %all-to-all-start.1 = ((bf16[8,12,4096]{2,1,0:T(8,128)(2,1)}), bf16[8,12,4096]{2,1,0:T(8,128)(2,1)S(1)}, u32[]{:S(2)}, u32[]{:S(2)}) async-start(bf16[8,12,4096]{2,1,0:T(8,128)(2,1)} %convert_element_type.72), calls=%async_computation.3 | async-start | bytes 2097152 | tf_op jit(solution)/shard_map/all_to_all | solution.py:173
  422.1 25.4 %all-to-all-done.1 = bf16[8,12,4096]{2,1,0:T(8,128)(2,1)S(1)} async-done(((bf16[8,12,4096]{2,1,0:T(8,128)(2,1)}), bf16[8,12,4096]{2,1,0:T(8,128)(2,1)S(1)}, u32[]{:S(2)}, u32[]{:S(2)}) %all-to-all-start.1) | async-done | bytes 786464 | tf_op jit(solution)/shard_map/all_to_all | solution.py:173
  448.8 2.9 gather_fusion
  453.4 2.9 multiply_reduce_fusion.1
  (238 shorter events, 117.1 us)
Async XLA Ops:
  7.2 10.8 %copy-start = (bf16[2048,544]{0,1:T(8,128)(2,1)S(1)}, bf16[2048,544]{0,1:T(8,128)(2,1)}, u32[]{:S(2)}) copy-start(bf16[2048,544]{0,1:T(8,128)(2,1)} %param.26) | copy-start | bytes 6684676
  7.2 46.1 %all-reduce.16.cloned.1.call-start = ((), (), s32[]{:S(2)}) async-start(), calls=%async_computation.4 | async-start | bytes 557056 | tf_op jit(solution)/shard_map/psum | solution.py:88
  8.1 6.3 %collective-permute-start = (bf16[3,2048]{1,0:T(4,128)(2,1)S(1)}, bf16[3,2048]{1,0:T(4,128)(2,1)S(1)}, u32[]{:S(2)}, u32[]{:S(2)}) collective-permute-start(bf16[3,2048]{1,0:T(4,128)(2,1)S(1)} %slice.130), channel_id=1, source_target_pairs={{0,4},{4,8},{8,12},{12,16},{16,20},{20,24},{24,28},{1,5},{5,9},{9,... | collective-permute-start | bytes 36872 | tf_op jit(solution)/shard_map/ppermute | solution.py:14
  15.7 37.6 %copy-start.19 = (f32[2048]{0:T(1024)S(1)}, f32[2048]{0:T(1024)}, u32[]{:S(2)}) copy-start(f32[2048]{0:T(1024)} %param.28) | copy-start | bytes 24580
  19.4 132.7 %all-gather.6.cloned.1.call-start = ((), (), s32[]{:S(2)}) async-start(), calls=%async_computation.6 | async-start | bytes 1179648 | tf_op jit(solution)/shard_map/all_gather | solution.py:19
  100.1 7.1 %copy-start.9 = (f32[1,16,2048]{2,1,0:T(8,128)S(1)}, f32[1,16,2048]{2,1,0:T(8,128)}, u32[]{:S(2)}) copy-start(f32[1,16,2048]{2,1,0:T(8,128)} %slice.154) | copy-start | bytes 393220
  111.4 82.4 %all-gather.4.cloned.1.call-start = ((), (), s32[]{:S(2)}) async-start(), calls=%async_computation.5 | async-start | bytes 1179648 | tf_op jit(solution)/shard_map/all_gather | solution.py:19
  116.6 165.9 %reduce-scatter.3.cloned.1.call-start = ((), (), s32[]{:S(2)}) async-start(), calls=%async_computation.7 | async-start | bytes 2621440 | tf_op jit(solution)/shard_map/reduce_scatter | solution.py:128
  116.7 11.8 %copy-start.3 = (f32[8,16,2048]{2,1,0:T(8,128)S(1)}, f32[8,16,2048]{2,1,0:T(8,128)}, u32[]{:S(2)}) copy-start(f32[8,16,2048]{2,1,0:T(8,128)} %pad.102) | copy-start | bytes 3145732
  121.4 9.4 %copy-start.4 = (f32[8,16,2048]{2,1,0:T(8,128)S(1)}, f32[8,16,2048]{2,1,0:T(8,128)}, u32[]{:S(2)}) copy-start(f32[8,16,2048]{2,1,0:T(8,128)} %pad.45) | copy-start | bytes 3145732
  130.8 63.1 %copy-start.6 = (f32[7,16,2048]{2,1,0:T(8,128)S(1)}, f32[7,16,2048]{2,1,0:T(8,128)}, u32[]{:S(2)}) copy-start(f32[7,16,2048]{2,1,0:T(8,128)} %slice_add_fusion.5) | copy-start | bytes 2752516
  195.3 38.8 %copy-start.8 = (bf16[128,2048]{1,0:T(8,128)(2,1)S(1)}, bf16[128,2048]{1,0:T(8,128)(2,1)}, u32[]{:S(2)}) copy-start(bf16[128,2048]{1,0:T(8,128)(2,1)} %param.23) | copy-start | bytes 1572868
  195.3 38.8 %copy-start.13 = (f32[1,2048]{1,0:T(1,128)S(1)}, f32[1,2048]{1,0:T(1,128)}, u32[]{:S(2)}) copy-start(f32[1,2048]{1,0:T(1,128)} %copy-done.12) | copy-start | bytes 24580
  195.3 38.8 %copy-start.15 = (f32[1,2048]{1,0:T(1,128)S(1)}, f32[1,2048]{1,0:T(1,128)}, u32[]{:S(2)}) copy-start(f32[1,2048]{1,0:T(1,128)} %copy-done.14) | copy-start | bytes 24580
  195.3 38.8 %copy-start.16 = (f32[2048]{0:T(1024)S(1)}, f32[2048]{0:T(1024)}, u32[]{:S(2)}) copy-start(f32[2048]{0:T(1024)} %param.25) | copy-start | bytes 24580
  195.3 38.8 %copy-start.20 = (f32[2048]{0:T(1024)S(1)}, f32[2048]{0:T(1024)}, u32[]{:S(2)}) copy-start(f32[2048]{0:T(1024)} %param.30) | copy-start | bytes 24580
  235.1 9.6 %copy-start.18 = (s32[32,2]{0,1:T(2,128)S(1)}, s32[32,2]{0,1:T(2,128)}, u32[]{:S(2)}) copy-start(s32[32,2]{0,1:T(2,128)} %param.34) | copy-start | bytes 772
  235.1 47.3 %copy-start.10 = (bf16[32,4096]{1,0:T(8,128)(2,1)S(1)}, bf16[32,4096]{1,0:T(8,128)(2,1)}, u32[]{:S(2)}) copy-start(bf16[32,4096]{1,0:T(8,128)(2,1)} %param.32) | copy-start | bytes 786436
  244.6 39.7 %copy-start.17 = (f32[4096]{0:T(1024)S(1)}, f32[4096]{0:T(1024)}, u32[]{:S(2)}) copy-start(f32[4096]{0:T(1024)} %param.33) | copy-start | bytes 49156
  244.7 99.3 %all-gather.8.cloned.1.call-start = ((), (), s32[]{:S(2)}) async-start(), calls=%async_computation.8 | async-start | bytes 3932160 | tf_op jit(solution)/shard_map/all_gather | solution.py:163
  317.2 96.8 %reduce-scatter.5.cloned.1.call-start = ((), (), s32[]{:S(2)}) async-start(), calls=%async_computation.9 | async-start | bytes 3932160 | tf_op jit(solution)/shard_map/reduce_scatter | solution.py:167
  375.9 46.1 %copy-start.21 = (f32[32,2]{0,1:T(2,128)S(1)}, f32[32,2]{0,1:T(2,128)}, u32[]{:S(2)}) copy-start(f32[32,2]{0,1:T(2,128)} %param.35) | copy-start | bytes 772
  416.2 31.3 %all-to-all-start.1 = ((bf16[8,12,4096]{2,1,0:T(8,128)(2,1)}), bf16[8,12,4096]{2,1,0:T(8,128)(2,1)S(1)}, u32[]{:S(2)}, u32[]{:S(2)}) async-start(bf16[8,12,4096]{2,1,0:T(8,128)(2,1)} %convert_element_type.72), calls=%async_computation.3 | async-start | bytes 2097152 | tf_op jit(solution)/shard_map/all_to_all | solution.py:173
  448.8 9.1 %copy-start.1 = (bf16[2048,544]{0,1:T(8,128)(2,1)S(1)}, bf16[2048,544]{0,1:T(8,128)(2,1)}, u32[]{:S(2)}) copy-start(bf16[2048,544]{0,1:T(8,128)(2,1)} %param.26) | copy-start | bytes 6684676
  (6 other events, 14.0 us)
Sparse Core Ops, SparseCore 0:
  19.5 33.7 all-reduce.15
  111.5 40.5 all-gather.5
  154.8 38.8 all-gather.3
  244.8 37.5 reduce-scatter.2
  317.3 26.5 all-gather.7
  376.0 37.9 reduce-scatter.4
where the time goes:
time: 467 us; the launch traced here: 465 us
  waiting for transfers between devices  223 us (48%)
  local copies, waits for them, and re-layouts  88.8 us (19%)
  other arithmetic  49.3 us (11%)
  matrix products  46.1 us (10%)
  blocking collectives  31.1 us (7%)
  between operations  14.6 us (3%)
  starting transfers between devices  10.9 us (2%)
    all_gather x2, waiting for transfers between devices, prefix(): gathered = jax.tree.map(lambda a: lax.all_gather(a, axis), part)  61.9 us
    reduce_scatter x1, waiting for transfers between devices, per_device(): lax.psum_scatter(expert_share(arrived_flat, up_weight, down_weight).astyp...  38.1 us
    reduce_scatter x1, waiting for transfers between devices, per_device(): lax.psum_scatter(jnp.dot(mixed, out_weight, preferred_element_type=jnp.fl...  36.9 us
    psum x1, waiting for transfers between devices, per_device(): lax.psum(jnp.dot(inner, x_weight, preferred_element_type=jnp.float32), 'tp')  33.8 us
    all_to_all x1, blocking collectives, per_device(): lax.all_to_all(along_seq, 'seq', split_axis=0, concat_axis=0, tiled=True)  31.1 us
    mul x48, local copies, waits for them, and re-layouts, advance(): entry_row[:, :, None] * drive_row[:, None, :]  28.5 us
    all_gather x1, waiting for transfers between devices, per_device(): lax.all_gather(arrived_seq.reshape(1, seq_count * capacity, width), 'tp',...  26.5 us
    all_to_all x1, waiting for transfers between devices, per_device(): lax.all_to_all(summed.reshape(seq_count, capacity, width).astype(jnp.bflo...  25.4 us
  transfers between devices with their start and end apart: 8, of which 8 were waited for; matrix products, arithmetic and copies ran while one was open for 5% of the time, Pallas kernels for 0%

commit v1 on v0

--- a/solution.py
+++ b/solution.py
@@ -85,7 +85,9 @@
         )
     )
     inner = jax.nn.silu(conv_out).astype(jnp.bfloat16)
-    projected = lax.psum(jnp.dot(inner, x_weight, preferred_element_type=jnp.float32), "tp")
+    projected = jnp.sum(
+        lax.all_gather(jnp.dot(inner, x_weight, preferred_element_type=jnp.float32), "tp"), axis=0
+    )
     dt_low = projected[:, :DTRANK].astype(jnp.bfloat16)
     entry_rows = projected[:, DTRANK : DTRANK + STATE]
     readout_rows = projected[:, DTRANK + STATE :]

time: 467 us -> 457 us (0.979)
  waiting for transfers between devices: 223 us -> 208 us
    psum x1 -> x0, waiting for transfers between devices: 33.8 us -> none  [per_device(): lax.psum(jnp.dot(inner, x_weight, preferred_element_type=jnp.float32), 'tp')]
    all_gather x0 -> x1, waiting for transfers between devices: none -> 19.3 us  [per_device(): lax.all_gather(jnp.dot(inner, x_weight, preferred_element_type=jnp.float3...]
where the time goes in v1:
time: 457 us; the launch traced here: 455 us
  waiting for transfers between devices  208 us (46%)
  local copies, waits for them, and re-layouts  92.6 us (20%)
  other arithmetic  50.2 us (11%)
  matrix products  46 us (10%)
  blocking collectives  31.1 us (7%)
  between operations  14.6 us (3%)
  starting transfers between devices  10.9 us (2%)
    all_gather x2, waiting for transfers between devices, prefix(): gathered = jax.tree.map(lambda a: lax.all_gather(a, axis), part)  61.4 us
    reduce_scatter x1, waiting for transfers between devices, per_device(): lax.psum_scatter(expert_share(arrived_flat, up_weight, down_weight).astyp...  38.1 us
    reduce_scatter x1, waiting for transfers between devices, per_device(): lax.psum_scatter(jnp.dot(mixed, out_weight, preferred_element_type=jnp.fl...  36.9 us
    all_to_all x1, blocking collectives, per_device(): lax.all_to_all(along_seq, 'seq', split_axis=0, concat_axis=0, tiled=True)  31.1 us
    mul x48, local copies, waits for them, and re-layouts, advance(): entry_row[:, :, None] * drive_row[:, None, :]  28.4 us
    all_gather x1, waiting for transfers between devices, per_device(): lax.all_gather(arrived_seq.reshape(1, seq_count * capacity, width), 'tp',...  26.5 us
    all_to_all x1, waiting for transfers between devices, per_device(): lax.all_to_all(summed.reshape(seq_count, capacity, width).astype(jnp.bflo...  25.4 us
    all_gather x1, waiting for transfers between devices, per_device(): lax.all_gather(jnp.dot(inner, x_weight, preferred_element_type=jnp.float3...  19.3 us
  transfers between devices with their start and end apart: 8, of which 8 were waited for; matrix products, arithmetic and copies ran while one was open for 5% of the time, Pallas kernels for 0%

profile of v1, /device:TPU:0, one launch (start us, length us, event | category | flops | bytes accessed | tf_op | source)
XLA Modules:
  0.0 454.6 jit_solution(4166044561626022139)
XLA Ops:
  8.1 4.9 %collective-permute-start = (bf16[3,2048]{1,0:T(4,128)(2,1)S(1)}, bf16[3,2048]{1,0:T(4,128)(2,1)S(1)}, u32[]{:S(2)}, u32[]{:S(2)}) collective-permute-start(bf16[3,2048]{1,0:T(4,128)(2,1)S(1)} %slice.130), channel_id=1, source_target_pairs={{0,4},{4,8},{8,12},{12,16},{16,20},{20,24},{24,28},{1,5},{5,9},{9,... | collective-permute-start | bytes 36872 | tf_op jit(solution)/shard_map/ppermute | solution.py:14
  19.4 19.3 %all-gather.12.cloned.1.call-done = f32[512,544]{0,1:T(8,128)} async-done(((f32[128,544]{0,1:T(8,128)}), f32[512,544]{0,1:T(8,128)}) %all-gather.12.cloned.1.call-update) | async-done | bytes 1114128 | tf_op jit(solution)/shard_map/all_gather | solution.py:89
  38.7 2.6 reshape.152
  44.5 2.7 convert_multiply_fusion.2
  47.8 2.6 copy_bitcast_fusion
  50.6 22.9 %while.37 = (s32[]{:T(128)}, f32[8,16,2048]{2,1,0:T(8,128)S(1)}, f32[16,8,2048]{2,1,0:T(8,128)}, f32[16,2048]{1,0:T(8,128)S(1)}, f32[16,8,16]{2,1,0:T(8,128)S(1)...) while((s32[]{:T(128)}, f32[8,16,2048]{2,1,0:T(8,128)S(1)}, f32[16,8,2048]{2,1,0:T(8,128)}, ...), condition=%wide.region_3.4_spmd.clone, body=%wide.region_2.3_spmd.clone.sunk | while | flops 1310723 | bytes 2623079 | solution.py:44
  84.4 4.2 pad.102
  106.8 2.5 pad.45
  109.3 4.1 pad.67
  114.3 4.1 pad.44
  122.0 19.8 %all-gather.8.cloned.1.call-done = f32[8,16,2048]{2,1,0:T(8,128)} async-done(((f32[1,16,2048]{2,1,0:T(8,128)}), f32[8,16,2048]{2,1,0:T(8,128)}) %all-gather.8.cloned.1.call-update) | async-done | bytes 1048592 | tf_op jit(solution)/shard_map/all_gather | solution.py:19
  141.8 41.6 %all-gather.6.cloned.1.call-done = f32[8,16,2048]{2,1,0:T(8,128)} async-done(((f32[1,16,2048]{2,1,0:T(8,128)}), f32[8,16,2048]{2,1,0:T(8,128)}) %all-gather.6.cloned.1.call-update) | async-done | bytes 1048592 | tf_op jit(solution)/shard_map/all_gather | solution.py:19
  185.0 37.0 %while.36 = (s32[]{:T(128)}, f32[8,16,2048]{2,1,0:T(8,128)S(1)}, f32[16,8,2048]{2,1,0:T(8,128)}, f32[16,8,2048]{2,1,0:T(8,128)}, f32[16,2048]{1,0:T(8,128)S(1)},...) while((s32[]{:T(128)}, f32[8,16,2048]{2,1,0:T(8,128)S(1)}, ...), condition=%wide.region_8.9_spmd, body=%wide.region_6.8_spmd.sunk | while | flops 1556482 | bytes 2821733 | solution.py:44
  225.0 9.5 %fusion.40 = f32[128,4096]{1,0:T(8,128)} fusion(bf16[128,2048]{1,0:T(8,128)(2,1)S(1)} %fusion.4, bf16[2048,4096]{1,0:T(8,128)(2,1)} %param.31), kind=kOutput, calls=%fused_computation.108 | convolution fusion | flops 2147483648 | bytes 19398656 | tf_op jit(solution)/shard_map/dot_general | solution.py:131
  235.4 36.9 %reduce-scatter.3.cloned.1.call-done = f32[32,4096]{1,0:T(8,128)} async-done(((f32[128,4096]{1,0:T(8,128)}), f32[32,4096]{1,0:T(8,128)}) %reduce-scatter.3.cloned.1.call-update) | async-done | bytes 524304 | tf_op jit(solution)/shard_map/reduce_scatter | solution.py:130
  274.8 31.1 %all_to_all.10 = bf16[8,12,4096]{2,1,0:T(8,128)(2,1)S(1)} all-to-all(bf16[8,12,4096]{2,1,0:T(8,128)(2,1)S(1)} %reshape_broadcast_in_dim_reshape.3), channel_id=1, replica_groups=mesh['seq'=8,'tp'=4] {'seq'}, dimensions={0} | all-to-all | bytes 1572864 | tf_op jit(solution)/shard_map/all_to_all | solution.py:164
  307.3 26.5 %all-gather.10.cloned.1.call-done = bf16[4,96,4096]{2,1,0:T(8,128)(2,1)} async-done(((bf16[1,96,4096]{2,1,0:T(8,128)(2,1)}), bf16[4,96,4096]{2,1,0:T(8,128)(2,1)}) %all-gather.10.cloned.1.call-update) | async-done | bytes 3145744 | tf_op jit(solution)/shard_map/all_gather | solution.py:165
  333.8 16.0 %multiply_convert_fusion.5 = bf16[384,3072]{1,0:T(8,128)(2,1)S(1)} fusion(bf16[384,4096]{1,0:T(8,128)(2,1)} %bitcast.99, bf16[4096,3072]{1,0:T(8,128)(2,1)} %param.36), kind=kOutput, calls=%fused_computation.16.clone.clone.1 | convolution fusion | flops 9669574656 | bytes 30670848 | tf_op jit(solution)/shard_map/dot_general | solution.py:53
  349.8 15.9 %convolution_convert_fusion = bf16[384,4096]{1,0:T(8,128)(2,1)} fusion(bf16[3072,4096]{1,0:T(8,128)(2,1)} %param.37, bf16[384,3072]{1,0:T(8,128)(2,1)S(1)} %multiply_convert_fusion.5), kind=kOutput, calls=%fused_computation.15 | convolution fusion | flops 9665249280 | bytes 30670848 | tf_op jit(solution)/shard_map/dot_general | solution.py:55
  365.7 38.1 %reduce-scatter.5.cloned.1.call-done = bf16[96,4096]{1,0:T(8,128)(2,1)} async-done(((bf16[384,4096]{1,0:T(8,128)(2,1)}), bf16[96,4096]{1,0:T(8,128)(2,1)}) %reduce-scatter.5.cloned.1.call-update) | async-done | bytes 786448 | tf_op jit(solution)/shard_map/reduce_scatter | solution.py:169
  406.0 5.5 %all-to-all-start.1 = ((bf16[8,12,4096]{2,1,0:T(8,128)(2,1)}), bf16[8,12,4096]{2,1,0:T(8,128)(2,1)S(1)}, u32[]{:S(2)}, u32[]{:S(2)}) async-start(bf16[8,12,4096]{2,1,0:T(8,128)(2,1)} %convert_element_type.72), calls=%async_computation.3 | async-start | bytes 2097152 | tf_op jit(solution)/shard_map/all_to_all | solution.py:175
  412.0 25.4 %all-to-all-done.1 = bf16[8,12,4096]{2,1,0:T(8,128)(2,1)S(1)} async-done(((bf16[8,12,4096]{2,1,0:T(8,128)(2,1)}), bf16[8,12,4096]{2,1,0:T(8,128)(2,1)S(1)}, u32[]{:S(2)}, u32[]{:S(2)}) %all-to-all-start.1) | async-done | bytes 786464 | tf_op jit(solution)/shard_map/all_to_all | solution.py:175
  438.7 2.9 gather_fusion
  443.2 2.9 multiply_reduce_fusion.1
  (251 shorter events, 120.0 us)
Async XLA Ops:
  7.2 10.7 %copy-start = (bf16[2048,544]{0,1:T(8,128)(2,1)S(1)}, bf16[2048,544]{0,1:T(8,128)(2,1)}, u32[]{:S(2)}) copy-start(bf16[2048,544]{0,1:T(8,128)(2,1)} %param.26) | copy-start | bytes 6684676
  7.2 31.5 %all-gather.12.cloned.1.call-start = ((), (), s32[]{:S(2)}) async-start(), calls=%async_computation.9 | async-start | bytes 1392640 | tf_op jit(solution)/shard_map/all_gather | solution.py:89
  8.1 6.3 %collective-permute-start = (bf16[3,2048]{1,0:T(4,128)(2,1)S(1)}, bf16[3,2048]{1,0:T(4,128)(2,1)S(1)}, u32[]{:S(2)}, u32[]{:S(2)}) collective-permute-start(bf16[3,2048]{1,0:T(4,128)(2,1)S(1)} %slice.130), channel_id=1, source_target_pairs={{0,4},{4,8},{8,12},{12,16},{16,20},{20,24},{24,28},{1,5},{5,9},{9,... | collective-permute-start | bytes 36872 | tf_op jit(solution)/shard_map/ppermute | solution.py:14
  19.3 25.2 %copy-start.24 = (f32[2048]{0:T(1024)S(1)}, f32[2048]{0:T(1024)}, u32[]{:S(2)}) copy-start(f32[2048]{0:T(1024)} %param.28) | copy-start | bytes 24580
  19.3 122.5 %all-gather.8.cloned.1.call-start = ((), (), s32[]{:S(2)}) async-start(), calls=%async_computation.5 | async-start | bytes 1179648 | tf_op jit(solution)/shard_map/all_gather | solution.py:19
  73.6 33.2 %copy-start.2 = (f32[8,16,2048]{2,1,0:T(8,128)}, f32[8,16,2048]{2,1,0:T(8,128)S(1)}, u32[]{:S(2)}) copy-start(f32[8,16,2048]{2,1,0:T(8,128)S(1)} %multiply_exponential_fusion) | copy-start | bytes 3145732
  101.5 81.9 %all-gather.6.cloned.1.call-start = ((), (), s32[]{:S(2)}) async-start(), calls=%async_computation.4 | async-start | bytes 1179648 | tf_op jit(solution)/shard_map/all_gather | solution.py:19
  102.8 10.7 %copy-start.10 = (f32[3,16,2048]{2,1,0:T(8,128)S(1)}, f32[3,16,2048]{2,1,0:T(8,128)}, u32[]{:S(2)}) copy-start(f32[3,16,2048]{2,1,0:T(8,128)} %get-tuple-element.250) | copy-start | bytes 1179652
  106.7 165.5 %reduce-scatter.3.cloned.1.call-start = ((), (), s32[]{:S(2)}) async-start(), calls=%async_computation.6 | async-start | bytes 2621440 | tf_op jit(solution)/shard_map/reduce_scatter | solution.py:130
  109.3 9.1 %copy-start.21 = (f32[128,16]{0,1:T(8,128)S(1)}, f32[128,16]{0,1:T(8,128)}, u32[]{:S(2)}) copy-start(f32[128,16]{0,1:T(8,128)} %get-tuple-element.260) | copy-start | bytes 24580
  109.3 9.3 %copy-start.5 = (f32[8,16,2048]{2,1,0:T(8,128)S(1)}, f32[8,16,2048]{2,1,0:T(8,128)}, u32[]{:S(2)}) copy-start(f32[8,16,2048]{2,1,0:T(8,128)} %pad.102) | copy-start | bytes 3145732
  121.0 62.7 %copy-start.8 = (f32[7,16,2048]{2,1,0:T(8,128)S(1)}, f32[7,16,2048]{2,1,0:T(8,128)}, u32[]{:S(2)}) copy-start(f32[7,16,2048]{2,1,0:T(8,128)} %slice_add_fusion.5) | copy-start | bytes 2752516
  185.0 39.0 %copy-start.17 = (f32[1,2048]{1,0:T(1,128)S(1)}, f32[1,2048]{1,0:T(1,128)}, u32[]{:S(2)}) copy-start(f32[1,2048]{1,0:T(1,128)} %copy-done.16) | copy-start | bytes 24580
  185.0 39.0 %copy-start.19 = (f32[1,2048]{1,0:T(1,128)S(1)}, f32[1,2048]{1,0:T(1,128)}, u32[]{:S(2)}) copy-start(f32[1,2048]{1,0:T(1,128)} %copy-done.18) | copy-start | bytes 24580
  185.0 39.0 %copy-start.20 = (f32[2048]{0:T(1024)S(1)}, f32[2048]{0:T(1024)}, u32[]{:S(2)}) copy-start(f32[2048]{0:T(1024)} %param.25) | copy-start | bytes 24580
  185.0 39.0 %copy-start.25 = (f32[2048]{0:T(1024)S(1)}, f32[2048]{0:T(1024)}, u32[]{:S(2)}) copy-start(f32[2048]{0:T(1024)} %param.30) | copy-start | bytes 24580
  225.0 9.6 %copy-start.23 = (s32[32,2]{0,1:T(2,128)S(1)}, s32[32,2]{0,1:T(2,128)}, u32[]{:S(2)}) copy-start(s32[32,2]{0,1:T(2,128)} %param.34) | copy-start | bytes 772
  234.5 37.8 %copy-start.14 = (bf16[32,4096]{1,0:T(8,128)(2,1)S(1)}, bf16[32,4096]{1,0:T(8,128)(2,1)}, u32[]{:S(2)}) copy-start(bf16[32,4096]{1,0:T(8,128)(2,1)} %param.32) | copy-start | bytes 786436
  234.5 39.8 %copy-start.22 = (f32[4096]{0:T(1024)S(1)}, f32[4096]{0:T(1024)}, u32[]{:S(2)}) copy-start(f32[4096]{0:T(1024)} %param.33) | copy-start | bytes 49156
  234.5 99.3 %all-gather.10.cloned.1.call-start = ((), (), s32[]{:S(2)}) async-start(), calls=%async_computation.7 | async-start | bytes 3932160 | tf_op jit(solution)/shard_map/all_gather | solution.py:165
  307.0 96.9 %reduce-scatter.5.cloned.1.call-start = ((), (), s32[]{:S(2)}) async-start(), calls=%async_computation.8 | async-start | bytes 3932160 | tf_op jit(solution)/shard_map/reduce_scatter | solution.py:169
  365.7 46.1 %copy-start.26 = (f32[32,2]{0,1:T(2,128)S(1)}, f32[32,2]{0,1:T(2,128)}, u32[]{:S(2)}) copy-start(f32[32,2]{0,1:T(2,128)} %param.35) | copy-start | bytes 772
  406.0 31.3 %all-to-all-start.1 = ((bf16[8,12,4096]{2,1,0:T(8,128)(2,1)}), bf16[8,12,4096]{2,1,0:T(8,128)(2,1)S(1)}, u32[]{:S(2)}, u32[]{:S(2)}) async-start(bf16[8,12,4096]{2,1,0:T(8,128)(2,1)} %convert_element_type.72), calls=%async_computation.3 | async-start | bytes 2097152 | tf_op jit(solution)/shard_map/all_to_all | solution.py:175
  438.7 9.1 %copy-start.1 = (bf16[2048,544]{0,1:T(8,128)(2,1)S(1)}, bf16[2048,544]{0,1:T(8,128)(2,1)}, u32[]{:S(2)}) copy-start(bf16[2048,544]{0,1:T(8,128)(2,1)} %param.26) | copy-start | bytes 6684676
  (12 other events, 38.7 us)
Sparse Core Ops, SparseCore 0:
  19.5 19.2 all-gather.11
  101.6 40.1 all-gather.7
  144.5 38.8 all-gather.5
  234.6 37.6 reduce-scatter.2
  307.1 26.5 all-gather.9
  365.9 37.9 reduce-scatter.4
